TPU v7x, 256 devices: a whole 4x4x8 slice. The times are simulated.
256 devices in a mesh: row: 64 (over y, z, core), col: 4 (over x).
Axes of the slice: x: 4, y: 4, z: 8, core: 2. Of those that a mesh axis runs over, the one named last changes fastest.
Arguments:
- features: bfloat16 [65536, 256], P('row', 'col'), may hold values from -600 to 600
- tile_vals: bfloat16 [10240, 128, 128], P('row'), may hold values from -0.125 to 0.125
- tile_rows: int32 [64, 160], P('row'), may hold values from 0 to 7
- tile_srcs: int32 [64, 160], P('row'), may hold values from 0 to 135, as said below
- tile_count: int32 [64], P('row'), may hold values from 20 to 160, as said below
- needed: int32 [64, 64, 2], P('row'), may hold values from 0 to 7, as said below
- hop_noise: float32 [2, 65536, 256], P(None, 'row', 'col'), may hold values from -0.24 to 0.24
- enc_weight: bfloat16 [3, 256, 256], replicated, may hold values from -3.59375 to 3.59375
Outputs:
- encoded: bfloat16 [65536, 256], P('row', 'col')
Inputs may be any that keep to these rules, and one draw needn't show every extreme that they name: `tile_count`: some row index has exactly 160 live slots; slots at or beyond a row index's count are ignored. `tile_srcs`: A value s below 8 names the row index's own block s; otherwise s = 8 + o * 2 + c names entry c of needed for owner o, and o is never the row index itself. needed[d, o, :] are 2 distinct block indices among owner o's 8 blocks.
All inputs are finite; a program needn't handle non-finite values.
Results may differ from a plain program's by a relative error of at most 0.0053.
Values may be sent and summed in bfloat16 or wider, within the bound.
No kernel may reach another device: no remote copies, remote signals or barrier semaphores. Data moves between devices by JAX's collectives and lax.ppermute only.
A program may use at most 64 MiB of HBM per device.

v0:
```python
import jax
import jax.numpy as jnp
from jax import lax
from jax.sharding import PartitionSpec as P

BLK = 128
BPD = 8
TPD = 160
CAP = 2
HOPS = 2


epsilon = 1e-06


def shards(features, tile_vals, tile_rows, tile_srcs, tile_count, needed, hop_noise, enc_weight):
    row_count = lax.axis_size("row")
    row_index = lax.axis_index("row")
    col_index = lax.axis_index("col")
    local_rows, local_width = features.shape
    sources = tile_srcs[0]
    block_rows = tile_rows[0]
    live_count = tile_count[0]
    wanted = needed[0]
    tile_order = jnp.arange(TPD, dtype=jnp.int32)
    onehot = (
        (block_rows[:, None] == jnp.arange(BPD, dtype=jnp.int32)[None, :])
        & (tile_order < live_count)[:, None]
    ).astype(jnp.float32)

    def normalize(values):
        squares = lax.psum(jnp.sum(values * values, axis=1), "col")
        return (values / jnp.sqrt(squares + epsilon)[:, None]).astype(jnp.bfloat16)

    remote = jnp.maximum(sources - BPD, 0)
    slot_table = wanted.reshape(-1)
    looked_up = jnp.sum(
        jnp.where(
            remote[:, None] == jnp.arange(row_count * CAP, dtype=jnp.int32)[None, :],
            slot_table[None, :],
            0,
        ),
        axis=1,
    )
    global_block = jnp.where(
        sources < BPD, row_index * BPD + sources, remote // CAP * BPD + looked_up
    )
    current = normalize(features.astype(jnp.float32))
    layers = [current]
    for hop_index in range(HOPS):
        whole = lax.all_gather(current.reshape(BPD, BLK * local_width), "row", axis=0, tiled=True)
        products = jnp.einsum(
            "tij,tjf->tif",
            tile_vals,
            jnp.take(whole, global_block, axis=0).reshape(TPD, BLK, local_width),
            preferred_element_type=jnp.float32,
        )
        summed = jnp.einsum("tr,tif->rif", onehot, products, precision=lax.Precision.HIGHEST)
        current = normalize(summed.reshape(local_rows, local_width) + hop_noise[hop_index])
        layers.append(current)
    stacked = jnp.stack(layers)
    weight_slice = lax.dynamic_slice_in_dim(
        enc_weight, col_index * local_width, local_width, axis=1
    )
    terms = jnp.einsum("kri,kio->ro", stacked, weight_slice, preferred_element_type=jnp.float32)
    encoded = lax.psum_scatter(terms, "col", scatter_dimension=1, tiled=True)
    return encoded.astype(jnp.bfloat16)


def solution(mesh):
    in_specs = (
        P("row", "col"),
        P("row", None, None),
        P("row", None),
        P("row", None),
        P("row"),
        P("row", None, None),
        P(None, "row", "col"),
        P(),
    )
    out_specs = P("row", "col")
    return jax.shard_map(shards, mesh=mesh, in_specs=in_specs, out_specs=out_specs, check_vma=False)
```

profile of v0, /device:TPU:1, one launch (start us, length us, event | category | flops | bytes accessed | tf_op | source)
XLA Modules:
  0.0 299.0 jit_solution(14227140690207375910)
XLA Ops:
  6.5 1.0 fusion.9
  7.5 9.3 %psum.21 = f32[1024]{0:T(1024)S(1)} all-reduce(f32[1024]{0:T(1024)S(1)} %fusion.9), channel_id=1, replica_groups=mesh['row'=64,'col'=4] {'col'}, use_global_device_ids=true, to_apply=%region_1.2 | all-reduce | flops 1024 | bytes 8192 | tf_op jit(solution)/shard_map/psum | solution.py:32
  16.8 0.9 fusion.10
  18.0 0.9 reshape.66
  19.0 0.8 copy.14
  20.5 1.0 slice_bitcast_fusion.1
  21.5 0.8 copy.24
  22.3 0.5 iota_compare_fusion.2
  22.8 0.7 compare_reduce_fusion
  23.5 0.7 add_maximum_fusion
  24.4 80.9 %all-gather.3.cloned.1.call-done = bf16[512,8192]{1,0:T(8,128)(2,1)} async-done(((bf16[8,8192]{1,0:T(8,128)(2,1)}), bf16[512,8192]{1,0:T(8,128)(2,1)}) %all-gather.3.cloned.1.call-update) | async-done | bytes 8388624 | tf_op jit(solution)/shard_map/all_gather | solution.py:51
  105.3 9.0 %gather_fusion = bf16[160,8192]{1,0:T(8,128)(2,1)S(1)} fusion(bf16[512,8192]{1,0:T(8,128)(2,1)} %all-gather.3.cloned.1.call-done, s32[1024]{0:T(1024)S(1)} %pad_clamp_fusion), kind=kCustom, calls=%fused_computation.clone | custom fusion | bytes 5243520 | tf_op jit(solution)/shard_map/jit(_take)/gather | solution.py:55
  114.4 1.8 broadcast_select_fusion.1
  116.2 8.4 %reshape.67 = bf16[160,128,64]{2,1,0:T(8,128)(2,1)} reshape(bf16[160,8192]{1,0:T(8,128)(2,1)} %broadcast_select_fusion.1) | data formatting | bytes 5242880 | tf_op jit(solution)/shard_map/reshape | solution.py:55
  124.6 7.7 %convolution_bitcast_fusion.1 = f32[160,128,64]{1,2,0:T(8,128)S(1)} fusion(bf16[160,128,64]{2,1,0:T(8,128)(2,1)} %reshape.67, bf16[160,128,128]{2,1,0:T(8,128)(2,1)} %param.11), kind=kOutput, calls=%fused_computation.9 | convolution fusion | flops 335544320 | bytes 13107200 | tf_op jit(solution)/shard_map/tij,tjf->tif/dot_general | solution.py:52
  132.4 4.7 %fusion.14 = (f32[8,128]{1,0:T(8,128)S(1)}, f32[8,128,64]{1,0,2:T(8,128)S(1)}) fusion(f32[8,8,8,128]{3,2,1,0:T(8,128)S(1)} %copy-done.3, f32[160,128,64]{1,2,0:T(8,128)S(1)} %convolution_bitcast_fusion.1, s32[160]{0:T(256)S(1)} %bitcast.59, pred[160]{0:T(512)(128)(4,1)S(1)} %copy-done.8), kind=kOutput, calls=%fused_computation.25 | convolution fusion | flops 126027264 | bytes 5772064 | tf_op jit(solution)/shard_map/tr,tif->rif/dot_general | solution.py:58
  137.4 8.4 %psum.22 = f32[1024]{0:T(1024)S(1)} all-reduce(f32[1024]{0:T(1024)S(1)} %bitcast.55), channel_id=1, replica_groups=mesh['row'=64,'col'=4] {'col'}, use_global_device_ids=true, to_apply=%region_4.6 | all-reduce | flops 1024 | bytes 8192 | tf_op jit(solution)/shard_map/psum | solution.py:32
  145.8 0.7 divide_convert_fusion.2
  147.5 0.7 divide_convert_fusion.1
  148.2 0.3 reduce-scatter.2.cloned.1.call-start
  148.5 0.7 fusion.31
  149.2 0.8 copy.25
  149.9 78.1 %all-gather.5.cloned.1.call-done = bf16[512,8192]{1,0:T(8,128)(2,1)} async-done(((bf16[8,8192]{1,0:T(8,128)(2,1)}), bf16[512,8192]{1,0:T(8,128)(2,1)}) %all-gather.5.cloned.1.call-update) | async-done | bytes 8388624 | tf_op jit(solution)/shard_map/all_gather | solution.py:51
  228.0 9.0 %gather_fusion.1 = bf16[160,8192]{1,0:T(8,128)(2,1)S(1)} fusion(bf16[512,8192]{1,0:T(8,128)(2,1)} %all-gather.5.cloned.1.call-done, s32[1024]{0:T(1024)S(1)} %pad_clamp_fusion), kind=kCustom, calls=%fused_computation.1.clone | custom fusion | bytes 5243520 | tf_op jit(solution)/shard_map/jit(_take)/gather | solution.py:55
  237.1 1.8 broadcast_select_fusion
  238.9 8.4 %reshape.70 = bf16[160,128,64]{2,1,0:T(8,128)(2,1)} reshape(bf16[160,8192]{1,0:T(8,128)(2,1)} %broadcast_select_fusion) | data formatting | bytes 5242880 | tf_op jit(solution)/shard_map/reshape | solution.py:55
  247.3 7.7 %convolution_bitcast_fusion = f32[160,128,64]{1,2,0:T(8,128)S(1)} fusion(bf16[160,128,64]{2,1,0:T(8,128)(2,1)} %reshape.70, bf16[160,128,128]{2,1,0:T(8,128)(2,1)} %param.11), kind=kOutput, calls=%fused_computation.8 | convolution fusion | flops 335544320 | bytes 13107200 | tf_op jit(solution)/shard_map/tij,tjf->tif/dot_general | solution.py:52
  255.1 4.7 %fusion.12 = (f32[8,128]{1,0:T(8,128)S(1)}, f32[8,128,64]{1,0,2:T(8,128)S(1)}) fusion(f32[8,8,8,128]{3,2,1,0:T(8,128)S(1)} %copy-done.4, f32[160,128,64]{1,2,0:T(8,128)S(1)} %convolution_bitcast_fusion, s32[160]{0:T(256)S(1)} %bitcast.60, pred[160]{0:T(512)(128)(4,1)S(1)} %copy-done.9), kind=kOutput, calls=%fused_computation.22 | convolution fusion | flops 126027264 | bytes 5772064 | tf_op jit(solution)/shard_map/tr,tif->rif/dot_general | solution.py:58
  259.9 8.4 %psum.23 = f32[1024]{0:T(1024)S(1)} all-reduce(f32[1024]{0:T(1024)S(1)} %bitcast.56), channel_id=1, replica_groups=mesh['row'=64,'col'=4] {'col'}, use_global_device_ids=true, to_apply=%region_6.8 | all-reduce | flops 1024 | bytes 8192 | tf_op jit(solution)/shard_map/psum | solution.py:32
  268.4 1.3 convolution_bitcast_fusion.2
  269.7 21.2 %reduce-scatter.2.cloned.1.call-done = f32[1024,64]{0,1:T(8,128)} async-done(((f32[1024,256]{0,1:T(8,128)}), f32[1024,64]{0,1:T(8,128)}) %reduce-scatter.2.cloned.1.call-update) | async-done | bytes 262160 | tf_op jit(solution)/shard_map/reduce_scatter | solution.py:66
  290.9 1.6 convert_element_type.26
  (42 shorter events, 2.0 us)
Async XLA Ops:
  6.5 261.8 %copy-start = (bf16[3,256,256]{2,1,0:T(8,128)(2,1)S(1)}, bf16[3,256,256]{2,1,0:T(8,128)(2,1)}, u32[]{:S(2)}) copy-start(bf16[3,256,256]{2,1,0:T(8,128)(2,1)} %param.17) | copy-start | bytes 1179652
  6.5 98.8 %all-gather.3.cloned.1.call-start = ((), (), s32[]{:S(2)}) async-start(), calls=%async_computation.1 | async-start | bytes 8519680 | tf_op jit(solution)/shard_map/all_gather | solution.py:51
  18.9 209.1 %all-gather.5.cloned.1.call-start = ((), (), s32[]{:S(2)}) async-start(), calls=%async_computation.2 | async-start | bytes 8519680 | tf_op jit(solution)/shard_map/all_gather | solution.py:51
  124.6 7.7 %copy-start.3 = (f32[8,8,8,128]{3,2,1,0:T(8,128)S(1)}, f32[8,8,8,128]{3,2,1,0:T(8,128)}, u32[]{:S(2)}) copy-start(f32[8,8,8,128]{3,2,1,0:T(8,128)} %copy.24) | copy-start | bytes 786436
  124.6 7.7 %copy-start.7 = (s32[1,160]{1,0:T(1,128)S(1)}, s32[1,160]{1,0:T(1,128)}, u32[]{:S(2)}) copy-start(s32[1,160]{1,0:T(1,128)} %param.12) | copy-start | bytes 1924
  124.6 7.7 %copy-start.8 = (pred[160]{0:T(512)(128)(4,1)S(1)}, pred[160]{0:T(512)(128)(4,1)}, u32[]{:S(2)}) copy-start(pred[160]{0:T(512)(128)(4,1)} %iota_compare_fusion.2) | copy-start | bytes 484
  132.3 13.5 %copy-start.1 = (f32[2,1024,64]{1,2,0:T(8,128)S(1)}, f32[2,1024,64]{1,2,0:T(8,128)}, u32[]{:S(2)}) copy-start(f32[2,1024,64]{1,2,0:T(8,128)} %param.16) | copy-start | bytes 1572868
  132.4 16.1 %copy-start.2 = (bf16[1024,64]{0,1:T(8,128)(2,1)S(1)}, bf16[1024,64]{0,1:T(8,128)(2,1)}, u32[]{:S(2)}) copy-start(bf16[1024,64]{0,1:T(8,128)(2,1)} %param.10) | copy-start | bytes 393220
  148.2 142.7 %reduce-scatter.2.cloned.1.call-start = ((), (), s32[]{:S(2)}) async-start(), calls=%async_computation.3 | async-start | bytes 1310720 | tf_op jit(solution)/shard_map/reduce_scatter | solution.py:66
  247.3 7.7 %copy-start.4 = (f32[8,8,8,128]{3,2,1,0:T(8,128)S(1)}, f32[8,8,8,128]{3,2,1,0:T(8,128)}, u32[]{:S(2)}) copy-start(f32[8,8,8,128]{3,2,1,0:T(8,128)} %copy.25) | copy-start | bytes 786436
  247.3 7.7 %copy-start.9 = (pred[160]{0:T(512)(128)(4,1)S(1)}, pred[160]{0:T(512)(128)(4,1)}, u32[]{:S(2)}) copy-start(pred[160]{0:T(512)(128)(4,1)} %iota_compare_fusion.2) | copy-start | bytes 484
  255.0 13.3 %copy-start.5 = (bf16[1,1024,64]{1,2,0:T(8,128)(2,1)S(1)}, bf16[1,1024,64]{1,2,0:T(8,128)(2,1)}, u32[]{:S(2)}) copy-start(bf16[1,1024,64]{1,2,0:T(8,128)(2,1)} %fusion.31) | copy-start | bytes 393220
  255.1 13.3 %copy-start.6 = (bf16[1,1024,64]{1,2,0:T(8,128)(2,1)S(1)}, bf16[1,1024,64]{1,2,0:T(8,128)(2,1)}, u32[]{:S(2)}) copy-start(bf16[1,1024,64]{1,2,0:T(8,128)(2,1)} %get-tuple-element.8) | copy-start | bytes 393220
Sparse Core Ops, SparseCore 0:
  19.0 86.2 all-gather.2
  148.3 79.6 all-gather.4
  269.8 21.0 reduce-scatter.1
where the time goes:
time: 300 us; the launch traced here: 299 us
  waiting for transfers between devices  180 us (60%)
  local copies, waits for them, and re-layouts  40.7 us (14%)
  matrix products  26.2 us (9%)
  blocking collectives  26.1 us (9%)
  between operations  14 us (5%)
  other arithmetic  11.5 us (4%)
    all_gather x2, waiting for transfers between devices, shards(): lax.all_gather(current.reshape(BPD, BLK * local_width), 'row', axis=0, ti...  159 us
    psum x3, blocking collectives, normalize(): squares = lax.psum(jnp.sum(values * values, axis=1), 'col')  26.1 us
    reduce_scatter x1, waiting for transfers between devices, shards(): encoded = lax.psum_scatter(terms, 'col', scatter_dimension=1, tiled=True)  21.2 us
    gather x2, local copies, waits for them, and re-layouts, shards(): jnp.take(whole, global_block, axis=0).reshape(TPD, BLK, local_width)  18.1 us
    reshape x2, local copies, waits for them, and re-layouts, shards(): jnp.take(whole, global_block, axis=0).reshape(TPD, BLK, local_width)  16.8 us
    dot_general x2, matrix products, shards(): jnp.einsum('tij,tjf->tif', tile_vals, jnp.take(whole, global_block, axis=...  15.4 us
    dot_general x2, matrix products, shards(): jnp.einsum('tr,tif->rif', onehot, products, precision=lax.Precision.HIGHEST)  9.47 us
  transfers between devices with their start and end apart: 3, of which 3 were waited for; matrix products, arithmetic and copies ran while one was open for 2% of the time, Pallas kernels for 0%

commit v1 on v0

v1 whole, which is shorter than its diff:
```python
import functools

import jax
import jax.numpy as jnp
import numpy as np
from jax import lax
from jax.experimental import pallas as pl
from jax.experimental.pallas import tpu as pltpu
from jax.sharding import Mesh, PartitionSpec as P

BLK = 128
BPD = 8
TPD = 160
PAIRS = BPD // 2
HOPS = 2
NY, NZ, NC, NX = 4, 8, 2, 4
WIDTH = 64
CHUNK = 16
GROUP = 4
EPS = 1e-06
bf16 = jnp.bfloat16
f32 = jnp.float32
VMEM = pltpu.VMEM
SMEM = pltpu.SMEM


def lane_low(shape):
    return lax.broadcasted_iota(jnp.int32, shape, len(shape) - 1) < WIDTH


def pair_squares(pair_values):
    total = jnp.zeros((BPD, BLK), f32)
    row = lax.broadcasted_iota(jnp.int32, (BPD, BLK), 0)
    half = lax.broadcasted_iota(jnp.int32, (BPD, BLK), 1) // WIDTH
    for p in range(PAIRS):
        v = pair_values[p]
        pick = jnp.where(row == 2 * p + half, 1.0, 0.0).astype(f32)
        total = total + lax.dot_general(
            pick, v * v, (((1,), (1,)), ((), ())),
            precision=lax.Precision.HIGHEST, preferred_element_type=f32,
        )
    return total


def row_scale(total):
    return (1.0 / jnp.sqrt(total + EPS)).T


def pair_scale(columns, p):
    return jnp.where(
        lane_low((BLK, BLK)),
        jnp.broadcast_to(columns[:, 2 * p : 2 * p + 1], (BLK, BLK)),
        jnp.broadcast_to(columns[:, 2 * p + 1 : 2 * p + 2], (BLK, BLK)),
    )


def swap_halves(v):
    return pltpu.roll(v, WIDTH, 1)


def join(low, high):
    return jnp.concatenate([low, high], axis=1)


def pack_kernel(feat_ref, out_ref, sq_ref):
    pairs = []
    for p in range(PAIRS):
        low = feat_ref[(2 * p) * BLK : (2 * p + 1) * BLK, :].astype(f32)
        high = feat_ref[(2 * p + 1) * BLK : (2 * p + 2) * BLK, :].astype(f32)
        pair = join(low, high)
        pairs.append(pair)
        for z in range(NZ):
            out_ref[z, p] = pair.astype(bf16)
    total = pair_squares(pairs)
    for i in range(NX * NZ):
        sq_ref[i] = total


def pick_kernel(me_ref, idx_ref, z_ref, sq_ref, out_ref, own_ref, norm):
    for z in range(NZ):
        total = sq_ref[z]
        for x in range(1, NX):
            total = total + sq_ref[x * NZ + z]
        columns = row_scale(total)
        for p in range(PAIRS):
            v = z_ref[z, p].astype(f32) * pair_scale(columns, p)
            norm[z, p] = v.astype(bf16)
            norm[z, PAIRS + p] = swap_halves(v).astype(bf16)
    own_ref[...] = norm[me_ref[0], 0:PAIRS]
    mask = lane_low((BLK, BLK))

    def body(i, carry):
        z = i % NZ
        first = idx_ref[2 * i]
        second = idx_ref[2 * i + 1]
        low = norm[z, first // 2 + PAIRS * (first % 2)]
        high = norm[z, second // 2 + PAIRS * (1 - second % 2)]
        out_ref[i] = jnp.where(mask, low, high)
        return carry

    lax.fori_loop(0, NY * NC * NZ, body, 0, unroll=2)


def tile_kernel(hop, rows_ref, srcs_ref, count_ref, tiles_ref, got_ref, own_ref, noise_ref, *rest):
    last = hop == HOPS - 1
    if last:
        out_ref, acc, tile_buf, src_buf, noise_buf, tile_sem, src_sem = rest
    else:
        out_ref, sq_ref, acc, tile_buf, src_buf, noise_buf, tile_sem, src_sem = rest
    count = count_ref[0]
    chunks = (count + CHUNK - 1) // CHUNK

    def tile_copy(c):
        return pltpu.make_async_copy(
            tiles_ref.at[pl.ds(c * CHUNK, CHUNK)], tile_buf.at[pl.ds(c * CHUNK, CHUNK)], tile_sem.at[c]
        )

    got_copy = pltpu.make_async_copy(got_ref, src_buf.at[pl.ds(0, NY * NC * NZ)], src_sem.at[0])
    own_copy = pltpu.make_async_copy(own_ref, src_buf.at[pl.ds(NY * NC * NZ, PAIRS)], src_sem.at[1])
    noise_copy = pltpu.make_async_copy(noise_ref.at[hop], noise_buf, src_sem.at[2])
    got_copy.start()
    own_copy.start()

    @pl.loop(0, chunks)
    def _(c):
        tile_copy(c).start()

    noise_copy.start()
    acc[...] = jnp.zeros_like(acc)
    got_copy.wait()
    own_copy.wait()

    def group(g, carry):
        @pl.when(g % (CHUNK // GROUP) == 0)
        def _():
            tile_copy(g // (CHUNK // GROUP)).wait()

        for j in range(GROUP):
            t = g * GROUP + j
            s = srcs_ref[t]
            o = (s - BPD) // 2
            y = o // (NZ * NC)
            z = (o // NC) % NZ
            k = o % NC
            slab = jnp.where(s < BPD, NY * NC * NZ + s // 2, (y * NC + k) * NZ + z)
            target = jnp.where(t < count, rows_ref[t] * 2 + s % 2, 2 * BPD)
            acc[target] += jnp.dot(tile_buf[t], src_buf[slab], preferred_element_type=f32)
        return carry

    lax.fori_loop(0, (count + GROUP - 1) // GROUP, group, 0)

    noise_copy.wait()
    mask = lane_low((BLK, BLK))
    pairs = []
    for p in range(PAIRS):
        noise = join(noise_buf[(2 * p) * BLK : (2 * p + 1) * BLK, :], noise_buf[(2 * p + 1) * BLK : (2 * p + 2) * BLK, :])
        u = noise + jnp.where(
            mask,
            acc[4 * p] + swap_halves(acc[4 * p + 1]),
            swap_halves(acc[4 * p + 2]) + acc[4 * p + 3],
        )
        pairs.append(u)
    total = pair_squares(pairs)
    if last:
        hi = total.astype(bf16).astype(f32)
        mid = (total - hi).astype(bf16).astype(f32)
        lo = total - hi - mid
        for x in range(NX):
            for p in range(PAIRS):
                out_ref[x, p * BLK : (p + 1) * BLK] = pairs[p].astype(bf16)
            out_ref[x, PAIRS * BLK : PAIRS * BLK + 16] = jnp.concatenate([hi, mid], axis=0).astype(bf16)
            out_ref[x, PAIRS * BLK + 16 : PAIRS * BLK + 32] = jnp.concatenate([lo, jnp.zeros_like(lo)], axis=0).astype(bf16)
    else:
        for p in range(PAIRS):
            for z in range(NZ):
                out_ref[z, p] = pairs[p].astype(bf16)
        for i in range(NX * NZ):
            sq_ref[i] = total


def early_kernel(h_ref, w_ref, out_ref):
    for p in range(PAIRS):
        total = jnp.zeros((BLK, BLK), f32)
        for k in range(HOPS):
            for x in range(NX):
                total = total + jnp.dot(h_ref[x, k, p], w_ref[k, x], preferred_element_type=f32)
        out_ref[p] = total


def final_kernel(got_ref, w_ref, early_ref, out_ref):
    total = jnp.zeros((BPD, BLK), f32)
    for x in range(NX):
        a = got_ref[x, PAIRS * BLK : PAIRS * BLK + 16].astype(f32)
        b = got_ref[x, PAIRS * BLK + 16 : PAIRS * BLK + 32].astype(f32)
        total = total + (a[:BPD] + a[BPD:] + b[:BPD])
    columns = row_scale(total)
    for p in range(PAIRS):
        raw = jnp.zeros((BLK, BLK), f32)
        for x in range(NX):
            raw = raw + jnp.dot(got_ref[x, p * BLK : (p + 1) * BLK], w_ref[HOPS, x], preferred_element_type=f32)
        v = early_ref[p] + raw * pair_scale(columns, p)
        out_ref[(2 * p) * BLK : (2 * p + 1) * BLK, :] = v[:, :WIDTH].astype(bf16)
        out_ref[(2 * p + 1) * BLK : (2 * p + 2) * BLK, :] = swap_halves(v)[:, :WIDTH].astype(bf16)


def whole(space=VMEM):
    return pl.BlockSpec(memory_space=space)


def call(kernel, name, in_specs, out_shape, scratch=(), limit=24 << 20, flops=1 << 20, moved=1 << 20, **kw):
    outs = jax.tree.map(lambda _: whole(), out_shape)
    return pl.pallas_call(
        kernel,
        name=name,
        out_shape=out_shape,
        in_specs=in_specs,
        out_specs=outs,
        scratch_shapes=list(scratch),
        compiler_params=pltpu.CompilerParams(vmem_limit_bytes=limit),
        cost_estimate=pl.CostEstimate(flops=flops, bytes_accessed=moved, transcendentals=0),
        **kw,
    )


def shape(dims, kind):
    return jax.ShapeDtypeStruct(dims, kind)


def shards(features, tile_vals, tile_rows, tile_srcs, tile_count, needed, hop_noise, enc_weight):
    z_index = lax.axis_index("z").astype(jnp.int32).reshape(1)
    x_index = lax.axis_index("x")

    packed, squares = call(
        pack_kernel, "pack", [whole()],
        (shape((NZ, PAIRS, BLK, BLK), bf16), shape((NX * NZ, BPD, BLK), f32)),
    )(features)
    wanted = needed.reshape(NY, NZ, NC, 2).transpose(0, 2, 1, 3).reshape(NY * NC, NZ * 2)
    wanted, packed = lax.optimization_barrier((wanted, packed))

    weights = lax.dynamic_slice_in_dim(enc_weight, x_index * WIDTH, WIDTH, axis=2).reshape(HOPS + 1, NX, WIDTH, WIDTH)
    nothing = jnp.zeros_like(weights)
    weights = jnp.concatenate(
        [jnp.concatenate([weights, nothing], axis=-1), jnp.concatenate([nothing, weights], axis=-1)], axis=-2
    )

    owned = []
    asked = None
    for hop in range(HOPS):
        last = hop == HOPS - 1
        along = lax.all_to_all(packed, "z", 0, 0, tiled=True)
        sums = lax.all_to_all(squares, ("x", "z"), 0, 0, tiled=True)
        if asked is None:
            asked = lax.all_to_all(wanted, ("y", "core"), 0, 0, tiled=True).reshape(-1)
        picked, own = call(
            pick_kernel, "pick", [whole(SMEM), whole(SMEM), whole(), whole()],
            (shape((NY * NC * NZ, BLK, BLK), bf16), shape((PAIRS, BLK, BLK), bf16)),
            [pltpu.VMEM((NZ, BPD, BLK, BLK), bf16)],
        )(z_index, asked, along, sums)
        owned.append(own)
        got = lax.all_to_all(picked, ("y", "core"), 0, 0, tiled=True)
        if last:
            both = jnp.stack(owned)
            spread = lax.all_to_all(
                jnp.broadcast_to(both[None], (NX,) + both.shape), "x", 0, 0, tiled=True
            )
            early = call(early_kernel, "early", [whole(), whole()], shape((PAIRS, BLK, BLK), f32))(spread, weights)
        scratch = [
            pltpu.VMEM((2 * BPD + 1, BLK, BLK), f32),
            pltpu.VMEM((TPD, BLK, BLK), bf16),
            pltpu.VMEM((NY * NC * NZ + PAIRS, BLK, BLK), bf16),
            pltpu.VMEM((BPD * BLK, WIDTH), f32),
            pltpu.SemaphoreType.DMA((TPD // CHUNK,)),
            pltpu.SemaphoreType.DMA((3,)),
        ]
        if last:
            outs = shape((NX, PAIRS * BLK + 32, BLK), bf16)
        else:
            outs = (
                shape((NZ, PAIRS, BLK, BLK), bf16),
                shape((NX * NZ, BPD, BLK), f32),
            )
        specs = [whole(SMEM)] * 3 + [whole(pl.ANY)] * 4
        result = call(
            functools.partial(tile_kernel, hop), "tiles", specs, outs, scratch, flops=TPD * 2 * BLK**3, moved=8 << 20,
        )(tile_rows.reshape(-1), tile_srcs.reshape(-1), tile_count, tile_vals, got, own, hop_noise)
        if last:
            tail = result
        else:
            packed, squares = result
    tail = lax.all_to_all(tail, "x", 0, 0, tiled=True)
    return call(final_kernel, "final", [whole(), whole(), whole()], shape((BPD * BLK, WIDTH), bf16))(tail, weights, early)


def solution(mesh):
    grid = Mesh(np.array(mesh.devices).reshape(NY, NZ, NC, NX), ("y", "z", "core", "x"))
    row = ("y", "z", "core")
    in_specs = (
        P(row, "x"),
        P(row, None, None),
        P(row, None),
        P(row, None),
        P(row),
        P(row, None, None),
        P(None, row, "x"),
        P(),
    )
    return jax.shard_map(shards, mesh=grid, in_specs=in_specs, out_specs=P(row, "x"), check_vma=False)
```

time: 300 us -> 242 us (0.81)
  waiting for transfers between devices: 180 us -> 84.4 us
  blocking collectives: 26.1 us -> 70.8 us
  Pallas kernels: 0 us -> 39.8 us
  matrix products: 26.2 us -> 0 us
  starting transfers between devices: 0.31 us -> 23.4 us
  local copies, waits for them, and re-layouts: 40.7 us -> 18.9 us
  between operations: 14 us -> 0.82 us
  other arithmetic: 11.5 us -> 2.48 us
    all_gather x2 -> x0, waiting for transfers between devices: 159 us -> none  [shards(): lax.all_gather(current.reshape(BPD, BLK * local_width), 'row', axis=0, ti...]
    all_to_all x0 -> x5, waiting for transfers between devices: none -> 84.4 us  [the longest x2 48.7 us: shards(): got = lax.all_to_all(picked, ('y', 'core'), 0, 0, tiled=True)]
    all_to_all x0 -> x4, blocking collectives: none -> 70.8 us  [the longest x2 32.2 us: shards(): sums = lax.all_to_all(squares, ('x', 'z'), 0, 0, tiled=True)]
    pallas_call x0 -> x7, Pallas kernels: none -> 39.8 us  [the longest x2 24.1 us: shards(): call(functools.partial(tile_kernel, hop), 'tiles', specs, outs, scratch,...]
    dot_general x5 -> x0, matrix products: 26.2 us -> none  [the longest x2 15.4 us: shards(): jnp.einsum('tij,tjf->tif', tile_vals, jnp.take(whole, global_block, axis=...]
    psum x3 -> x0, blocking collectives: 26.1 us -> none  [normalize(): squares = lax.psum(jnp.sum(values * values, axis=1), 'col')]
    all_to_all x0 -> x5, starting transfers between devices: none -> 23.4 us  [the longest x2 11.4 us: shards(): got = lax.all_to_all(picked, ('y', 'core'), 0, 0, tiled=True)]
    reduce_scatter x1 -> x0, waiting for transfers between devices: 21.2 us -> none  [shards(): encoded = lax.psum_scatter(terms, 'col', scatter_dimension=1, tiled=True)]
  transfers between devices with their start and end apart: 3 -> 5, of which waited for: 3 -> 4; matrix products, arithmetic and copies ran while one was open for 2% -> 2% of each run, Pallas kernels for 0% -> 6%
where the time goes in v1:
time: 242 us; the launch traced here: 241 us
  waiting for transfers between devices  84.4 us (35%)
  blocking collectives  70.8 us (29%)
  Pallas kernels  39.8 us (16%)
  starting transfers between devices  23.4 us (10%)
  local copies, waits for them, and re-layouts  18.9 us (8%)
  other arithmetic  2.48 us (1%)
    all_to_all x2, waiting for transfers between devices, shards(): got = lax.all_to_all(picked, ('y', 'core'), 0, 0, tiled=True)  48.7 us
    all_to_all x2, blocking collectives, shards(): sums = lax.all_to_all(squares, ('x', 'z'), 0, 0, tiled=True)  32.2 us
    all_to_all x1, blocking collectives, shards(): along = lax.all_to_all(packed, 'z', 0, 0, tiled=True)  28.3 us
    all_to_all x1, waiting for transfers between devices, shards(): along = lax.all_to_all(packed, 'z', 0, 0, tiled=True)  27.8 us
    pallas_call x2, Pallas kernels, shards(): call(functools.partial(tile_kernel, hop), 'tiles', specs, outs, scratch,...  24.1 us
    unnamed x26, local copies, waits for them, and re-layouts  14 us
    pallas_call x2, Pallas kernels, shards(): call(pick_kernel, 'pick', [whole(SMEM), whole(SMEM), whole(), whole()], (...  12.3 us
    all_to_all x2, starting transfers between devices, shards(): got = lax.all_to_all(picked, ('y', 'core'), 0, 0, tiled=True)  11.4 us
  transfers between devices with their start and end apart: 5, of which 4 were waited for; matrix products, arithmetic and copies ran while one was open for 2% of the time, Pallas kernels for 6%

profile of v1, /device:TPU:1, one launch (start us, length us, event | category | flops | bytes accessed | tf_op | source)
XLA Modules:
  0.0 240.5 jit_solution(7028797964656961238)
XLA Ops:
  0.0 1.1 copy.20.feat_ref
  1.1 1.3 pack.1
  2.4 0.8 reshape.30
  3.6 10.4 %all_to_all.49 = s32[8,1,16]{2,1,0:T(1,128)S(1)} all-to-all(s32[8,1,16]{2,1,0:T(1,128)S(1)} %bitcast.22), channel_id=1, replica_groups=mesh['y'=4,'z'=8,'core'=2,'x'=4] {'y','core'}, dimensions={0} | all-to-all | bytes 1024 | tf_op jit(solution)/shard_map/all_to_all | solution.py:253
  13.9 20.0 %all_to_all.50.sq_ref = f32[32,8,128]{2,1,0:T(8,128)S(1)} all-to-all(f32[32,8,128]{2,1,0:T(8,128)S(1)} %get-tuple-element.18), channel_id=1, replica_groups=mesh['y'=4,'z'=8,'core'=2,'x'=4] {'x','z'}, dimensions={0} | all-to-all | bytes 262144 | tf_op jit(solution)/shard_map/all_to_all | solution.py:251
  33.9 3.6 %all-to-all-start.1 = ((bf16[8,4,128,128]{3,2,1,0:T(8,128)(2,1)}), bf16[8,4,128,128]{3,2,1,0:T(8,128)(2,1)S(1)}, u32[]{:S(2)}, u32[]{:S(2)}) async-start(bf16[8,4,128,128]{3,2,1,0:T(8,128)(2,1)} %get-tuple-element.17), calls=%async_computation.1 | async-start | bytes 2097152 | tf_op jit(solution)/shard_map/all_to_all | solution.py:250
  38.8 27.8 %all-to-all-done.1.z_ref = bf16[8,4,128,128]{3,2,1,0:T(8,128)(2,1)S(1)} async-done(((bf16[8,4,128,128]{3,2,1,0:T(8,128)(2,1)}), bf16[8,4,128,128]{3,2,1,0:T(8,128)(2,1)S(1)}, u32[]{:S(2)}, u32[]{:S(2)}) %all-to-all-start.1) | async-done | bytes 1048608 | tf_op jit(solution)/shard_map/all_to_all | solution.py:250
  66.6 6.1 %pick.2 = (bf16[64,128,128]{2,1,0:T(8,128)(2,1)S(1)}, bf16[4,128,128]{2,1,0:T(8,128)(2,1)S(1)}) custom-call(s32[1]{0:T(128)} %bitcast.2.me_ref, s32[128]{0:T(128)S(1)} %reshape.32.idx_ref, bf16[8,4,128,128]{3,2,1,0:T(8,128)(2,1)S(1)} %all-to-all-done.1.z_ref, f32[32,8,128]{2,1,0:T(8,128)S(1)} %all_to_all.50.sq_ref), custom_call_target="tpu_custom_call" | custom-call | flops 1048576 | bytes 1048576 | tf_op jit(solution)/shard_map/pick/pallas_call | solution.py:254
  72.7 1.3 copy-done.5
  74.7 4.1 %all-to-all-start.3 = ((bf16[64,128,128]{2,1,0:T(8,128)(2,1)}), bf16[64,128,128]{2,1,0:T(8,128)(2,1)S(1)}, u32[]{:S(2)}, u32[]{:S(2)}) async-start(bf16[64,128,128]{2,1,0:T(8,128)(2,1)} %copy-done.5), calls=%async_computation.3 | async-start | bytes 4194304 | tf_op jit(solution)/shard_map/all_to_all | solution.py:260
  78.8 1.4 copy.22.noise_ref
  80.9 24.2 %all-to-all-done.3.got_ref = bf16[64,128,128]{2,1,0:T(8,128)(2,1)S(1)} async-done(((bf16[64,128,128]{2,1,0:T(8,128)(2,1)}), bf16[64,128,128]{2,1,0:T(8,128)(2,1)S(1)}, u32[]{:S(2)}, u32[]{:S(2)}) %all-to-all-start.3) | async-done | bytes 2097184 | tf_op jit(solution)/shard_map/all_to_all | solution.py:260
  105.1 2.5 %copy-done.1 = bf16[160,128,128]{2,1,0:T(8,128)(2,1)S(1)} copy-done((bf16[160,128,128]{2,1,0:T(8,128)(2,1)S(1)}, bf16[160,128,128]{2,1,0:T(8,128)(2,1)}, u32[]{:S(2)}) %copy-start.1) | copy-done | bytes 5242904
  107.6 0.9 copy-done.7
  108.5 12.1 %tiles.2 = (bf16[8,4,128,128]{3,2,1,0:T(8,128)(2,1)S(1)}, f32[32,8,128]{2,1,0:T(8,128)S(1)}) custom-call(s32[160]{0:T(256)S(1)} %bitcast.16, s32[160]{0:T(256)S(1)} %bitcast.18, s32[1]{0:T(128)S(6)} %copy.25.count_ref, bf16[160,128,128]{2,1,0:T(8,128)(2,1)S(1)} %copy-done.1, bf16[64,128,128]{2,1,0:T(8,128)(2,1)S(1)} %all-to-all-done.3.got_ref, ...), custom_call_target="tpu_custom_call" | custom-call | flops 671088640 | bytes 8388608 | tf_op jit(solution)/shard_map/tiles/pallas_call | solution.py:283
  120.5 12.2 %all_to_all.51.sq_ref = f32[32,8,128]{2,1,0:T(8,128)S(1)} all-to-all(f32[32,8,128]{2,1,0:T(8,128)S(1)} %get-tuple-element.22), channel_id=1, replica_groups=mesh['y'=4,'z'=8,'core'=2,'x'=4] {'x','z'}, dimensions={0} | all-to-all | bytes 262144 | tf_op jit(solution)/shard_map/all_to_all | solution.py:251
  132.8 28.3 %all_to_all.52.z_ref = bf16[8,4,128,128]{3,2,1,0:T(8,128)(2,1)S(1)} all-to-all(bf16[8,4,128,128]{3,2,1,0:T(8,128)(2,1)S(1)} %get-tuple-element.21), channel_id=1, replica_groups=mesh['y'=4,'z'=8,'core'=2,'x'=4] {'z'}, dimensions={0} | all-to-all | bytes 2097152 | tf_op jit(solution)/shard_map/all_to_all | solution.py:250
  161.1 6.1 %pick.3 = (bf16[64,128,128]{2,1,0:T(8,128)(2,1)S(1)}, bf16[4,128,128]{2,1,0:T(8,128)(2,1)S(1)}) custom-call(s32[1]{0:T(128)} %bitcast.2.me_ref, s32[128]{0:T(128)S(1)} %reshape.32.idx_ref, bf16[8,4,128,128]{3,2,1,0:T(8,128)(2,1)S(1)} %all_to_all.52.z_ref, f32[32,8,128]{2,1,0:T(8,128)S(1)} %all_to_all.51.sq_ref), custom_call_target="tpu_custom_call" | custom-call | flops 1048576 | bytes 1048576 | tf_op jit(solution)/shard_map/pick/pallas_call | solution.py:254
  167.2 1.3 copy-done.4
  169.2 7.3 %all-to-all-start.6 = ((bf16[64,128,128]{2,1,0:T(8,128)(2,1)}), bf16[64,128,128]{2,1,0:T(8,128)(2,1)S(1)}, u32[]{:S(2)}, u32[]{:S(2)}) async-start(bf16[64,128,128]{2,1,0:T(8,128)(2,1)} %copy-done.4), calls=%async_computation.6 | async-start | bytes 4194304 | tf_op jit(solution)/shard_map/all_to_all | solution.py:260
  176.5 1.7 pad_maximum_fusion
  178.2 24.5 %all-to-all-done.6.got_ref = bf16[64,128,128]{2,1,0:T(8,128)(2,1)S(1)} async-done(((bf16[64,128,128]{2,1,0:T(8,128)(2,1)}), bf16[64,128,128]{2,1,0:T(8,128)(2,1)S(1)}, u32[]{:S(2)}, u32[]{:S(2)}) %all-to-all-start.6) | async-done | bytes 2097184 | tf_op jit(solution)/shard_map/all_to_all | solution.py:260
  202.7 2.2 broadcast_in_dim.2
  204.9 4.2 %all-to-all-start.8 = ((bf16[4,2,4,128,128]{4,3,2,1,0:T(8,128)(2,1)}), bf16[4,2,4,128,128]{4,3,2,1,0:T(8,128)(2,1)}, u32[]{:S(2)}, u32[]{:S(2)}) async-start(bf16[4,2,4,128,128]{4,3,2,1,0:T(8,128)(2,1)} %broadcast_in_dim.2), calls=%async_computation.8 | async-start | bytes 2097152 | tf_op jit(solution)/shard_map/all_to_all | solution.py:263
  209.2 2.5 %copy-done.2 = bf16[160,128,128]{2,1,0:T(8,128)(2,1)S(1)} copy-done((bf16[160,128,128]{2,1,0:T(8,128)(2,1)S(1)}, bf16[160,128,128]{2,1,0:T(8,128)(2,1)}, u32[]{:S(2)}) %copy-start.2) | copy-done | bytes 5242904
  211.6 0.9 copy-done.9
  212.5 12.0 %tiles.3 = bf16[4,544,128]{2,1,0:T(8,128)(2,1)S(1)} custom-call(s32[160]{0:T(256)S(1)} %bitcast.17, s32[160]{0:T(256)S(1)} %bitcast.19, s32[1]{0:T(128)S(6)} %copy.25.count_ref, bf16[160,128,128]{2,1,0:T(8,128)(2,1)S(1)} %copy-done.2, bf16[64,128,128]{2,1,0:T(8,128)(2,1)S(1)} %all-to-all-done.6.got_ref, bf16[4,128,128]{2,1,0:T(8,128)(2,1)S(1)} %copy-done.9, ...), custom_call_target="tpu_custom_call" | custom-call | flops 671088640 | bytes 8388608 | tf_op jit(solution)/shard_map/tiles/pallas_call | solution.py:283
  224.6 0.8 copy-done.3
  225.4 4.2 %all-to-all-start.7 = ((bf16[4,544,128]{2,1,0:T(8,128)(2,1)}), bf16[4,544,128]{2,1,0:T(8,128)(2,1)S(1)}, u32[]{:S(2)}, u32[]{:S(2)}) async-start(bf16[4,544,128]{2,1,0:T(8,128)(2,1)} %copy-done.3), calls=%async_computation.7 | async-start | bytes 1114112 | tf_op jit(solution)/shard_map/all_to_all | solution.py:290
  229.8 1.6 early.1.early_ref
  231.5 7.8 %all-to-all-done.7.got_ref = bf16[4,544,128]{2,1,0:T(8,128)(2,1)S(1)} async-done(((bf16[4,544,128]{2,1,0:T(8,128)(2,1)}), bf16[4,544,128]{2,1,0:T(8,128)(2,1)S(1)}, u32[]{:S(2)}, u32[]{:S(2)}) %all-to-all-start.7) | async-done | bytes 557088 | tf_op jit(solution)/shard_map/all_to_all | solution.py:290
  239.7 0.8 copy.24
  (26 shorter events, 3.7 us)
Async XLA Ops:
  0.0 229.6 %copy-start = (bf16[3,256,256]{2,1,0:T(8,128)(2,1)S(1)}, bf16[3,256,256]{2,1,0:T(8,128)(2,1)}, u32[]{:S(2)}) copy-start(bf16[3,256,256]{2,1,0:T(8,128)(2,1)} %param.15) | copy-start | bytes 1179652
  33.9 32.7 %all-to-all-start.1 = ((bf16[8,4,128,128]{3,2,1,0:T(8,128)(2,1)}), bf16[8,4,128,128]{3,2,1,0:T(8,128)(2,1)S(1)}, u32[]{:S(2)}, u32[]{:S(2)}) async-start(bf16[8,4,128,128]{3,2,1,0:T(8,128)(2,1)} %get-tuple-element.17), calls=%async_computation.1 | async-start | bytes 2097152 | tf_op jit(solution)/shard_map/all_to_all | solution.py:250
  72.7 1.3 copy-start.5
  74.1 0.7 copy-start.6
  74.7 30.4 %copy-start.10 = (s32[1,160]{1,0:T(1,128)S(1)}, s32[1,160]{1,0:T(1,128)}, u32[]{:S(2)}) copy-start(s32[1,160]{1,0:T(1,128)} %param.10) | copy-start | bytes 1924
  74.7 30.4 %copy-start.11 = (s32[1,160]{1,0:T(1,128)S(1)}, s32[1,160]{1,0:T(1,128)}, u32[]{:S(2)}) copy-start(s32[1,160]{1,0:T(1,128)} %param.11) | copy-start | bytes 1924
  74.7 30.4 %all-to-all-start.3 = ((bf16[64,128,128]{2,1,0:T(8,128)(2,1)}), bf16[64,128,128]{2,1,0:T(8,128)(2,1)S(1)}, u32[]{:S(2)}, u32[]{:S(2)}) async-start(bf16[64,128,128]{2,1,0:T(8,128)(2,1)} %copy-done.5), calls=%async_computation.3 | async-start | bytes 4194304 | tf_op jit(solution)/shard_map/all_to_all | solution.py:260
  105.1 2.5 %copy-start.1 = (bf16[160,128,128]{2,1,0:T(8,128)(2,1)S(1)}, bf16[160,128,128]{2,1,0:T(8,128)(2,1)}, u32[]{:S(2)}) copy-start(bf16[160,128,128]{2,1,0:T(8,128)(2,1)} %tiles_ref.3) | copy-start | bytes 15728644
  107.6 0.9 copy-start.7
  167.2 1.3 copy-start.4
  168.5 0.7 copy-start.8
  169.2 33.5 %all-to-all-start.6 = ((bf16[64,128,128]{2,1,0:T(8,128)(2,1)}), bf16[64,128,128]{2,1,0:T(8,128)(2,1)S(1)}, u32[]{:S(2)}, u32[]{:S(2)}) async-start(bf16[64,128,128]{2,1,0:T(8,128)(2,1)} %copy-done.4), calls=%async_computation.6 | async-start | bytes 4194304 | tf_op jit(solution)/shard_map/all_to_all | solution.py:260
  204.9 20.5 %all-to-all-start.8 = ((bf16[4,2,4,128,128]{4,3,2,1,0:T(8,128)(2,1)}), bf16[4,2,4,128,128]{4,3,2,1,0:T(8,128)(2,1)}, u32[]{:S(2)}, u32[]{:S(2)}) async-start(bf16[4,2,4,128,128]{4,3,2,1,0:T(8,128)(2,1)} %broadcast_in_dim.2), calls=%async_computation.8 | async-start | bytes 2097152 | tf_op jit(solution)/shard_map/all_to_all | solution.py:263
  209.1 2.5 %copy-start.2 = (bf16[160,128,128]{2,1,0:T(8,128)(2,1)S(1)}, bf16[160,128,128]{2,1,0:T(8,128)(2,1)}, u32[]{:S(2)}) copy-start(bf16[160,128,128]{2,1,0:T(8,128)(2,1)} %tiles_ref.3) | copy-start | bytes 15728644
  211.6 0.9 copy-start.9
  224.6 0.8 copy-start.3
  225.4 13.9 %all-to-all-start.7 = ((bf16[4,544,128]{2,1,0:T(8,128)(2,1)}), bf16[4,544,128]{2,1,0:T(8,128)(2,1)S(1)}, u32[]{:S(2)}, u32[]{:S(2)}) async-start(bf16[4,544,128]{2,1,0:T(8,128)(2,1)} %copy-done.3), calls=%async_computation.7 | async-start | bytes 1114112 | tf_op jit(solution)/shard_map/all_to_all | solution.py:290

commit v2 on v1

v2 whole, which is shorter than its diff:
```python
import functools

import jax
import jax.numpy as jnp
import numpy as np
from jax import lax
from jax.experimental import pallas as pl
from jax.experimental.pallas import tpu as pltpu
from jax.sharding import Mesh, PartitionSpec as P

BLK = 128
BPD = 8
TPD = 160
PAIRS = BPD // 2
HOPS = 2
NY, NZ, NC, NX = 4, 8, 2, 4
WIDTH = 64
GROUP = 4
BUCKETS = 2 * BPD
MAXG = TPD // GROUP + BUCKETS
SLOTS = MAXG * GROUP
SHIFTS = (0, 1, 2, 3)
EPS = 1e-06
bf16 = jnp.bfloat16
f32 = jnp.float32
VMEM = pltpu.VMEM
SMEM = pltpu.SMEM
HBM = pltpu.HBM
DMA = pltpu.SemaphoreType.DMA


def lane_low(shape):
    return lax.broadcasted_iota(jnp.int32, shape, len(shape) - 1) < WIDTH


def pair_squares(pair_values):
    total = jnp.zeros((BPD, BLK), f32)
    row = lax.broadcasted_iota(jnp.int32, (BPD, BLK), 0)
    half = lax.broadcasted_iota(jnp.int32, (BPD, BLK), 1) // WIDTH
    for p in range(PAIRS):
        v = pair_values[p]
        pick = jnp.where(row == 2 * p + half, 1.0, 0.0).astype(f32)
        total = total + lax.dot_general(
            pick, v * v, (((1,), (1,)), ((), ())),
            precision=lax.Precision.HIGHEST, preferred_element_type=f32,
        )
    return total


def row_scale(total):
    return (1.0 / jnp.sqrt(total + EPS)).T


def pair_scale(columns, p):
    return jnp.where(
        lane_low((BLK, BLK)),
        jnp.broadcast_to(columns[:, 2 * p : 2 * p + 1], (BLK, BLK)),
        jnp.broadcast_to(columns[:, 2 * p + 1 : 2 * p + 2], (BLK, BLK)),
    )


def swap_halves(v):
    return pltpu.roll(v, WIDTH, 1)


def stacked_pair(ref, p):
    first = ref[:, (2 * p) * BLK : (2 * p + 1) * BLK].astype(f32)
    second = ref[:, (2 * p + 1) * BLK : (2 * p + 2) * BLK].astype(f32)
    return jnp.concatenate([first, second], axis=0)


def pack_kernel(feat_ref, out_ref, sq_ref, buf, sem):
    rows = []
    for p in range(PAIRS):
        stacked = stacked_pair(feat_ref, p)
        buf[p] = stacked.T.astype(bf16)
        squares = stacked * stacked
        rows.append(jnp.sum(squares[:WIDTH], axis=0, keepdims=True))
        rows.append(jnp.sum(squares[WIDTH:], axis=0, keepdims=True))
    sq_ref[...] = jnp.concatenate(rows, axis=0)
    copies = [pltpu.make_async_copy(buf, out_ref.at[z], sem.at[z]) for z in range(NZ)]
    for copy in copies:
        copy.start()
    for copy in copies:
        copy.wait()


def pick_kernel(me_ref, idx_ref, z_ref, sq_ref, out_ref, own_ref, norm, buf, sem):
    for z in range(NZ):
        columns = row_scale(sq_ref[z])
        for p in range(PAIRS):
            v = z_ref[z, p].astype(f32) * pair_scale(columns, p)
            norm[z, p] = v.astype(bf16)
            norm[z, PAIRS + p] = swap_halves(v).astype(bf16)
    own_ref[...] = norm[me_ref[1], 0:PAIRS]
    mask = lane_low((BLK, BLK))
    base = (me_ref[0] * NZ * NC + me_ref[2]) * 2
    copies = []
    for dest in range(NY * NC):
        for z in range(NZ):
            at = base + dest * (NY * NZ * NC * 2) + z * NC * 2
            first = idx_ref[at]
            second = idx_ref[at + 1]
            low = norm[z, first // 2 + PAIRS * (first % 2)]
            high = norm[z, second // 2 + PAIRS * (1 - second % 2)]
            buf[dest * NZ + z] = jnp.where(mask, low, high)
        copy = pltpu.make_async_copy(
            buf.at[pl.ds(dest * NZ, NZ)], out_ref.at[pl.ds(dest * NZ, NZ)], sem.at[dest]
        )
        copy.start()
        copies.append(copy)
    for copy in copies:
        copy.wait()


def order_kernel(rows_ref, srcs_ref, count_ref, tile_ref, slab_ref, into_ref, groups_ref, fill, begin):
    count = count_ref[0]

    @pl.loop(0, 2 * SLOTS)
    def _(i):
        tile_ref[i] = TPD
        slab_ref[i] = 0

    for b in range(2 * BUCKETS):
        fill[b] = 0

    def bucket_of(t):
        s = srcs_ref[t]
        return jnp.where(s < BPD, 0, BUCKETS) + rows_ref[t] * 2 + s % 2

    @pl.loop(0, count)
    def _(t):
        b = bucket_of(t)
        fill[b] = fill[b] + 1

    for kind in range(2):
        def place(b, group):
            size = (fill[kind * BUCKETS + b] + GROUP - 1) // GROUP
            begin[kind * BUCKETS + b] = (kind * MAXG + group) * GROUP

            @pl.loop(0, size)
            def _(i):
                into_ref[kind * MAXG + group + i] = b

            return group + size

        groups_ref[kind] = lax.fori_loop(0, BUCKETS, place, jnp.int32(0))

    @pl.loop(0, count)
    def _(t):
        b = bucket_of(t)
        at = begin[b]
        begin[b] = at + 1
        s = srcs_ref[t]
        o = (s - BPD) // 2
        y = o // (NZ * NC)
        z = (o // NC) % NZ
        k = o % NC
        tile_ref[at] = t
        slab_ref[at] = jnp.where(s < BPD, s // 2, (y * NC + k) * NZ + z)


def stage_kernel(tiles_ref, out_ref, sem):
    copy = pltpu.make_async_copy(tiles_ref, out_ref.at[pl.ds(0, TPD)], sem)
    copy.start()
    out_ref[TPD] = jnp.zeros((BLK, BLK), bf16)
    copy.wait()


def add_groups(kind, tile_ref, slab_ref, into_ref, groups_ref, tiles_ref, src_ref, acc):
    def group(g, carry):
        at = (kind * MAXG + g) * GROUP
        left = jnp.concatenate([tiles_ref[tile_ref[at + j]] for j in range(GROUP)], axis=1)
        right = jnp.concatenate([src_ref[slab_ref[at + j]] for j in range(GROUP)], axis=0)
        acc[into_ref[kind * MAXG + g]] += jnp.dot(left, right, preferred_element_type=f32)
        return carry

    lax.fori_loop(0, groups_ref[kind], group, 0)


def own_kernel(tile_ref, slab_ref, into_ref, groups_ref, tiles_ref, src_ref, acc_ref):
    acc_ref[...] = jnp.zeros_like(acc_ref)
    add_groups(0, tile_ref, slab_ref, into_ref, groups_ref, tiles_ref, src_ref, acc_ref)


def far_kernel(hop, tile_ref, slab_ref, into_ref, groups_ref, tiles_ref, src_ref, part_ref, noise_ref, *rest):
    last = hop == HOPS - 1
    if last:
        out_ref, acc, buf, sem = rest
    else:
        out_ref, sq_ref, acc, buf, sem = rest
    acc[...] = part_ref[...]
    add_groups(1, tile_ref, slab_ref, into_ref, groups_ref, tiles_ref, src_ref, acc)
    mask = lane_low((BLK, BLK))
    pairs = []
    for p in range(PAIRS):
        u = stacked_pair(noise_ref.at[hop], p).T + jnp.where(
            mask,
            acc[4 * p] + swap_halves(acc[4 * p + 1]),
            swap_halves(acc[4 * p + 2]) + acc[4 * p + 3],
        )
        pairs.append(u)
        buf[p * BLK : (p + 1) * BLK] = u.astype(bf16)
    total = pair_squares(pairs)
    if last:
        hi = total.astype(bf16).astype(f32)
        mid = (total - hi).astype(bf16).astype(f32)
        lo = total - hi - mid
        buf[PAIRS * BLK : PAIRS * BLK + 16] = jnp.concatenate([hi, mid], axis=0).astype(bf16)
        buf[PAIRS * BLK + 16 : PAIRS * BLK + 32] = jnp.concatenate([lo, jnp.zeros_like(lo)], axis=0).astype(bf16)
        copies = [pltpu.make_async_copy(buf, out_ref, sem.at[0])]
    else:
        sq_ref[...] = total
        copies = [pltpu.make_async_copy(buf, out_ref.at[z], sem.at[z]) for z in range(NZ)]
    for copy in copies:
        copy.start()
    for copy in copies:
        copy.wait()


def early_kernel(x_ref, w_ref, *refs):
    h_refs, out_ref = refs[:-1], refs[-1]
    for p in range(PAIRS):
        total = jnp.zeros((BLK, BLK), f32)
        for k in range(HOPS):
            for j, shift in enumerate(SHIFTS):
                source = (x_ref[0] + NX - shift) % NX
                total = total + jnp.dot(h_refs[k * NX + j][p], w_ref[k, source], preferred_element_type=f32)
        out_ref[p] = total


def final_kernel(x_ref, w_ref, early_ref, *refs):
    got_refs, out_ref = refs[:-1], refs[-1]
    total = jnp.zeros((BPD, BLK), f32)
    for got_ref in got_refs:
        a = got_ref[PAIRS * BLK : PAIRS * BLK + 16].astype(f32)
        b = got_ref[PAIRS * BLK + 16 : PAIRS * BLK + 32].astype(f32)
        total = total + (a[:BPD] + a[BPD:] + b[:BPD])
    columns = row_scale(total)
    for p in range(PAIRS):
        raw = jnp.zeros((BLK, BLK), f32)
        for j, shift in enumerate(SHIFTS):
            source = (x_ref[0] + NX - shift) % NX
            raw = raw + jnp.dot(got_refs[j][p * BLK : (p + 1) * BLK], w_ref[HOPS, source], preferred_element_type=f32)
        v = (early_ref[p] + raw * pair_scale(columns, p)).T
        out_ref[:, (2 * p) * BLK : (2 * p + 1) * BLK] = v[:WIDTH].astype(bf16)
        out_ref[:, (2 * p + 1) * BLK : (2 * p + 2) * BLK] = v[WIDTH:].astype(bf16)


def whole(space=VMEM):
    return pl.BlockSpec(memory_space=space)


def call(kernel, name, in_specs, outs, scratch=(), limit=24 << 20, flops=1 << 20, moved=1 << 20):
    shapes = [jax.ShapeDtypeStruct(dims, kind) for dims, kind, _ in outs]
    specs = [whole(space) for _, _, space in outs]
    single = len(outs) == 1
    return pl.pallas_call(
        kernel,
        name=name,
        out_shape=shapes[0] if single else shapes,
        in_specs=in_specs,
        out_specs=specs[0] if single else specs,
        scratch_shapes=list(scratch),
        compiler_params=pltpu.CompilerParams(vmem_limit_bytes=limit),
        cost_estimate=pl.CostEstimate(flops=flops, bytes_accessed=moved, transcendentals=0),
    )


def shift_x(value, shift):
    return lax.ppermute(value, "x", [(i, (i + shift) % NX) for i in range(NX)])


def shards(features, tile_vals, tile_rows, tile_srcs, tile_count, needed, hop_noise, enc_weight):
    me = jnp.stack([lax.axis_index("y"), lax.axis_index("z"), lax.axis_index("core")]).astype(jnp.int32)
    x_index = lax.axis_index("x").astype(jnp.int32)
    x_only = x_index.reshape(1)
    noise = hop_noise.transpose(0, 2, 1)

    packed, squares = call(
        pack_kernel, "pack", [whole()],
        [((NZ, PAIRS, BLK, BLK), bf16, HBM), ((BPD, BLK), f32, VMEM)],
        [VMEM((PAIRS, BLK, BLK), bf16), DMA((NZ,))],
    )(features.T)
    packed, squares, needed, rows, srcs, count, enc_weight, tile_vals = lax.optimization_barrier(
        (packed, squares, needed.reshape(-1), tile_rows.reshape(-1), tile_srcs.reshape(-1), tile_count, enc_weight, tile_vals)
    )

    weights = lax.dynamic_slice_in_dim(enc_weight, x_index * WIDTH, WIDTH, axis=2).reshape(HOPS + 1, NX, WIDTH, WIDTH)
    nothing = jnp.zeros_like(weights)
    weights = jnp.concatenate(
        [jnp.concatenate([weights, nothing], axis=-1), jnp.concatenate([nothing, weights], axis=-1)], axis=-2
    )
    lists = call(
        order_kernel, "order", [whole(SMEM)] * 3,
        [((2 * SLOTS,), jnp.int32, SMEM), ((2 * SLOTS,), jnp.int32, SMEM), ((2 * MAXG,), jnp.int32, SMEM), ((2,), jnp.int32, SMEM)],
        [SMEM((2 * BUCKETS,), jnp.int32), SMEM((2 * BUCKETS,), jnp.int32)],
    )(rows, srcs, count)
    staged = call(
        stage_kernel, "stage", [whole(HBM)], [((TPD + 1, BLK, BLK), bf16, VMEM)], [DMA(())], moved=10 << 20,
    )(tile_vals)

    spread = []
    asked = None
    for hop in range(HOPS):
        last = hop == HOPS - 1
        along = lax.all_to_all(packed.reshape(NZ, PAIRS, BLK, BLK), "z", 0, 0, tiled=True)
        sums = lax.all_gather(lax.psum(squares, "x"), "z", axis=0)
        if asked is None:
            asked = lax.all_gather(needed, ("y", "core"), axis=0).reshape(-1)
        picked, own = call(
            pick_kernel, "pick", [whole(SMEM), whole(SMEM), whole(), whole()],
            [((NY * NC * NZ, BLK, BLK), bf16, HBM), ((PAIRS, BLK, BLK), bf16, VMEM)],
            [VMEM((NZ, BPD, BLK, BLK), bf16), VMEM((NY * NC * NZ, BLK, BLK), bf16), DMA((NY * NC,))],
        )(me, asked, along, sums)
        got = lax.all_to_all(picked, ("y", "core"), 0, 0, tiled=True)
        part = call(
            own_kernel, "own", [whole(SMEM)] * 4 + [whole()] * 2, [((BUCKETS, BLK, BLK), f32, VMEM)],
            flops=TPD * 2 * BLK**3, moved=4 << 20,
        )(*lists, staged, own)
        spread += [own] + [shift_x(own, shift) for shift in SHIFTS[1:]]
        if last:
            early = call(
                early_kernel, "early", [whole(SMEM)] + [whole()] * (1 + 2 * NX), [((PAIRS, BLK, BLK), f32, VMEM)]
            )(x_only, weights, *spread)
        if last:
            outs = [((PAIRS * BLK + 32, BLK), bf16, HBM)]
            buf = VMEM((PAIRS * BLK + 32, BLK), bf16)
        else:
            outs = [((NZ, PAIRS * BLK, BLK), bf16, HBM), ((BPD, BLK), f32, VMEM)]
            buf = VMEM((PAIRS * BLK, BLK), bf16)
        result = call(
            functools.partial(far_kernel, hop), "far", [whole(SMEM)] * 4 + [whole()] * 4, outs,
            [VMEM((BUCKETS, BLK, BLK), f32), buf, DMA((NZ,))],
            flops=TPD * 2 * BLK**3, moved=8 << 20,
        )(*lists, staged, got, part, noise)
        if not last:
            packed, squares = result
    tails = [result] + [shift_x(result, shift) for shift in SHIFTS[1:]]
    return call(
        final_kernel, "final", [whole(SMEM)] + [whole()] * (2 + NX), [((WIDTH, BPD * BLK), bf16, VMEM)]
    )(x_only, weights, early, *tails).T


def solution(mesh):
    grid = Mesh(np.array(mesh.devices).reshape(NY, NZ, NC, NX), ("y", "z", "core", "x"))
    row = ("y", "z", "core")
    in_specs = (
        P(row, "x"),
        P(row, None, None),
        P(row, None),
        P(row, None),
        P(row),
        P(row, None, None),
        P(None, row, "x"),
        P(),
    )
    return jax.shard_map(shards, mesh=grid, in_specs=in_specs, out_specs=P(row, "x"), check_vma=False)
```

time: 242 us -> 221 us (0.913)
  waiting for transfers between devices: 84.4 us -> 30.4 us
  starting transfers between devices: 23.4 us -> 48 us
  blocking collectives: 70.8 us -> 78.5 us
  local copies, waits for them, and re-layouts: 18.9 us -> 22 us
    all_to_all x4 -> x0, blocking collectives: 70.8 us -> none  [the longest x2 32.2 us: shards(): sums = lax.all_to_all(squares, ('x', 'z'), 0, 0, tiled=True)]
    all_gather x0 -> x3, blocking collectives: none -> 62.7 us  [the longest x2 51.1 us: shards(): sums = lax.all_gather(lax.psum(squares, 'x'), 'z', axis=0)]
    all_to_all x3 -> x2, waiting for transfers between devices: 35.6 us -> 0.01 us  [shards(): lax.all_to_all(packed.reshape(NZ, PAIRS, BLK, BLK), 'z', 0, 0, tiled=True)]
    all_to_all x2, waiting for transfers between devices: 48.7 us -> 26 us  [shards(): got = lax.all_to_all(picked, ('y', 'core'), 0, 0, tiled=True)]
    psum x0 -> x2, blocking collectives: none -> 15.8 us  [shards(): sums = lax.all_gather(lax.psum(squares, 'x'), 'z', axis=0)]
    ppermute x0 -> x9, starting transfers between devices: none -> 11.1 us  [shift_x(): return lax.ppermute(value, 'x', [(i, (i + shift) % NX) for i in range(NX)])]
    unnamed x26 -> x43, local copies, waits for them, and re-layouts: 14 us -> 21.8 us
    all_to_all x2, starting transfers between devices: 11.4 us -> 19.2 us  [shards(): got = lax.all_to_all(picked, ('y', 'core'), 0, 0, tiled=True)]
  transfers between devices with their start and end apart: 5 -> 13, of which waited for: 4 -> 4; matrix products, arithmetic and copies ran while one was open for 2% -> 0% of each run, Pallas kernels for 6% -> 8%
where the time goes in v2:
time: 221 us; the launch traced here: 219 us
  blocking collectives  78.5 us (36%)
  starting transfers between devices  48 us (22%)
  Pallas kernels  38.6 us (17%)
  waiting for transfers between devices  30.4 us (14%)
  local copies, waits for them, and re-layouts  22 us (10%)
    all_gather x2, blocking collectives, shards(): sums = lax.all_gather(lax.psum(squares, 'x'), 'z', axis=0)  51.1 us
    all_to_all x2, waiting for transfers between devices, shards(): got = lax.all_to_all(picked, ('y', 'core'), 0, 0, tiled=True)  26 us
    unnamed x43, local copies, waits for them, and re-layouts  21.8 us
    all_to_all x2, starting transfers between devices, shards(): got = lax.all_to_all(picked, ('y', 'core'), 0, 0, tiled=True)  19.2 us
    all_to_all x2, starting transfers between devices, shards(): lax.all_to_all(packed.reshape(NZ, PAIRS, BLK, BLK), 'z', 0, 0, tiled=True)  17.8 us
    psum x2, blocking collectives, shards(): sums = lax.all_gather(lax.psum(squares, 'x'), 'z', axis=0)  15.8 us
    pallas_call x2, Pallas kernels, shards(): call(pick_kernel, 'pick', [whole(SMEM), whole(SMEM), whole(), whole()], [...  13.3 us
    all_gather x1, blocking collectives, shards(): asked = lax.all_gather(needed, ('y', 'core'), axis=0).reshape(-1)  11.6 us
  transfers between devices with their start and end apart: 13, of which 4 were waited for; matrix products, arithmetic and copies ran while one was open for 0% of the time, Pallas kernels for 8%

profile of v2, /device:TPU:1, one launch (start us, length us, event | category | flops | bytes accessed | tf_op | source)
XLA Modules:
  0.0 218.7 jit_solution(14333618471007637054)
XLA Ops:
  3.0 9.0 %all-to-all-start = ((bf16[8,4,128,128]{3,2,1,0:T(8,128)(2,1)}), bf16[8,4,128,128]{3,2,1,0:T(8,128)(2,1)S(1)}, u32[]{:S(2)}, u32[]{:S(2)}) async-start(bf16[8,4,128,128]{3,2,1,0:T(8,128)(2,1)} %get-tuple-element.29), calls=%async_computation | async-start | bytes 2097152 | tf_op jit(solution)/shard_map/all_to_all | solution.py:307
  12.0 11.6 %all-gather.1 = s32[8,1,128]{2,1,0:T(1,128)S(1)} all-gather(s32[1,1,128]{2,1,0:T(1,128)S(1)} %bitcast.26), channel_id=2, replica_groups=mesh['y'=4,'z'=8,'core'=2,'x'=4] {'y','core'}, dimensions={0}, use_global_device_ids=true | all-gather | bytes 4608 | tf_op jit(solution)/shard_map/all_gather | solution.py:310
  23.6 9.0 %psum.14 = f32[1,8,128]{2,1,0:T(8,128)S(1)} all-reduce(f32[1,8,128]{2,1,0:T(8,128)S(1)} %bitcast.21), channel_id=1, replica_groups=mesh['y'=4,'z'=8,'core'=2,'x'=4] {'x'}, use_global_device_ids=true, to_apply=%region_0.0 | all-reduce | flops 1024 | bytes 8192 | tf_op jit(solution)/shard_map/psum | solution.py:308
  32.6 20.5 %all_gather.21.sq_ref = f32[8,8,128]{2,1,0:T(8,128)S(1)} all-gather(f32[1,8,128]{2,1,0:T(8,128)S(1)} %psum.14), channel_id=1, replica_groups=mesh['y'=4,'z'=8,'core'=2,'x'=4] {'z'}, dimensions={0}, use_global_device_ids=true | all-gather | bytes 36864 | tf_op jit(solution)/shard_map/all_gather | solution.py:308
  53.2 6.6 %pick.2 = (bf16[64,128,128]{2,1,0:T(8,128)(2,1)S(1)}, bf16[4,128,128]{2,1,0:T(8,128)(2,1)}) custom-call(s32[3]{0:T(128)S(1)} %pad_add_fusion.me_ref, s32[1024]{0:T(1024)S(1)} %bitcast.19, bf16[8,4,128,128]{3,2,1,0:T(8,128)(2,1)S(1)} %all-to-all-done.z_ref, f32[8,8,128]{2,1,0:T(8,128)S(1)} %all_gather.21.sq_ref), custom_call_target="tpu_custom_call" | custom-call | flops 1048576 | bytes 1048576 | tf_op jit(solution)/shard_map/pick/pallas_call | solution.py:311
  59.9 1.3 copy-done.9
  61.2 10.7 %all-to-all-start.1 = ((bf16[64,128,128]{2,1,0:T(8,128)(2,1)}), bf16[64,128,128]{2,1,0:T(8,128)(2,1)S(1)}, u32[]{:S(2)}, u32[]{:S(2)}) async-start(bf16[64,128,128]{2,1,0:T(8,128)(2,1)} %copy-done.9), calls=%async_computation.1 | async-start | bytes 4194304 | tf_op jit(solution)/shard_map/all_to_all | solution.py:316
  72.6 2.5 %copy-done.5 = bf16[160,128,128]{2,1,0:T(8,128)(2,1)S(1)} copy-done((bf16[160,128,128]{2,1,0:T(8,128)(2,1)S(1)}, bf16[160,128,128]{2,1,0:T(8,128)(2,1)}, u32[]{:S(2)}) %copy-start.5) | copy-done | bytes 5242904
  75.7 6.8 %order.1 = (s32[448]{0:T(512)S(1)}, s32[448]{0:T(512)S(1)}, s32[112]{0:T(128)S(1)}, s32[2]{0:T(128)S(1)}) custom-call(s32[160]{0:T(256)S(1)} %bitcast.23, s32[160]{0:T(256)S(1)} %bitcast.24, s32[1]{0:T(128)S(6)} %copy.12.count_ref), custom_call_target="tpu_custom_call" | custom-call | flops 1048576 | bytes 1048576 | tf_op jit(solution)/shard_map/order/pallas_call | solution.py:294
  83.1 2.2 %own.2.part_ref = f32[16,128,128]{2,1,0:T(8,128)S(1)} custom-call(s32[448]{0:T(512)S(1)} %get-tuple-element.35.tile_ref, s32[448]{0:T(512)S(1)} %get-tuple-element.36.slab_ref, s32[112]{0:T(128)S(1)} %get-tuple-element.37.into_ref, s32[2]{0:T(128)S(1)} %get-tuple-element.38.groups_ref, bf16[161,128,128]{2,1,0:T(8,128)(2,1)S(1)} %stage.1.tiles_ref, ...), custom_call_target="tpu_custom_call" | custom-call | flops 671088640 | bytes 4194304 | tf_op jit(solution)/shard_map/own/pallas_call | solution.py:317
  85.4 2.3 %copy-done.1 = bf16[161,128,128]{2,1,0:T(8,128)(2,1)} copy-done((bf16[161,128,128]{2,1,0:T(8,128)(2,1)}, bf16[161,128,128]{2,1,0:T(8,128)(2,1)S(1)}, u32[]{:S(2)}) %copy-start.1) | copy-done | bytes 5275672
  87.7 10.4 %all-to-all-done.1.src_ref = bf16[64,128,128]{2,1,0:T(8,128)(2,1)S(1)} async-done(((bf16[64,128,128]{2,1,0:T(8,128)(2,1)}), bf16[64,128,128]{2,1,0:T(8,128)(2,1)S(1)}, u32[]{:S(2)}, u32[]{:S(2)}) %all-to-all-start.1) | async-done | bytes 2097184 | tf_op jit(solution)/shard_map/all_to_all | solution.py:316
  98.1 2.5 %copy-done.2 = bf16[161,128,128]{2,1,0:T(8,128)(2,1)S(1)} copy-done((bf16[161,128,128]{2,1,0:T(8,128)(2,1)S(1)}, bf16[161,128,128]{2,1,0:T(8,128)(2,1)}, u32[]{:S(2)}) %copy-start.2) | copy-done | bytes 5275672
  102.3 5.4 %far.2 = (bf16[8,512,128]{2,1,0:T(8,128)(2,1)S(1)}, f32[8,128]{1,0:T(8,128)S(1)}) custom-call(s32[448]{0:T(512)S(1)} %get-tuple-element.35.tile_ref, s32[448]{0:T(512)S(1)} %get-tuple-element.36.slab_ref, s32[112]{0:T(128)S(1)} %get-tuple-element.37.into_ref, s32[2]{0:T(128)S(1)} %copy-done.13, bf16[161,128,128]{2,1,0:T(8,128)(2,1)S(1)} %copy-done.2, ...), custom_call_target="tpu_custom_call" | custom-call | flops 671088640 | bytes 8388608 | tf_op jit(solution)/shard_map/far/pallas_call | solution.py:332
  109.3 8.8 %all-to-all-start.2 = ((bf16[8,4,128,128]{3,2,1,0:T(8,128)(2,1)}), bf16[8,4,128,128]{3,2,1,0:T(8,128)(2,1)S(1)}, u32[]{:S(2)}, u32[]{:S(2)}) async-start(bf16[8,4,128,128]{3,2,1,0:T(8,128)(2,1)} %bitcast.17), calls=%async_computation.2 | async-start | bytes 2097152 | tf_op jit(solution)/shard_map/all_to_all | solution.py:307
  118.1 6.8 %psum.15 = f32[1,8,128]{2,1,0:T(8,128)S(1)} all-reduce(f32[1,8,128]{2,1,0:T(8,128)S(1)} %bitcast.22), channel_id=1, replica_groups=mesh['y'=4,'z'=8,'core'=2,'x'=4] {'x'}, use_global_device_ids=true, to_apply=%region_1.0 | all-reduce | flops 1024 | bytes 8192 | tf_op jit(solution)/shard_map/psum | solution.py:308
  124.9 30.6 %all_gather.23.sq_ref = f32[8,8,128]{2,1,0:T(8,128)S(1)} all-gather(f32[1,8,128]{2,1,0:T(8,128)S(1)} %psum.15), channel_id=1, replica_groups=mesh['y'=4,'z'=8,'core'=2,'x'=4] {'z'}, dimensions={0}, use_global_device_ids=true | all-gather | bytes 36864 | tf_op jit(solution)/shard_map/all_gather | solution.py:308
  155.5 6.6 %pick.3 = (bf16[64,128,128]{2,1,0:T(8,128)(2,1)S(1)}, bf16[4,128,128]{2,1,0:T(8,128)(2,1)}) custom-call(s32[3]{0:T(128)S(1)} %copy-done.16, s32[1024]{0:T(1024)S(1)} %bitcast.20, bf16[8,4,128,128]{3,2,1,0:T(8,128)(2,1)S(1)} %all-to-all-done.2.z_ref, f32[8,8,128]{2,1,0:T(8,128)S(1)} %all_gather.23.sq_ref), custom_call_target="tpu_custom_call" | custom-call | flops 1048576 | bytes 1048576 | tf_op jit(solution)/shard_map/pick/pallas_call | solution.py:311
  162.2 1.3 copy-done.8
  163.5 8.4 %all-to-all-start.3 = ((bf16[64,128,128]{2,1,0:T(8,128)(2,1)}), bf16[64,128,128]{2,1,0:T(8,128)(2,1)S(1)}, u32[]{:S(2)}, u32[]{:S(2)}) async-start(bf16[64,128,128]{2,1,0:T(8,128)(2,1)} %copy-done.8), calls=%async_computation.3 | async-start | bytes 4194304 | tf_op jit(solution)/shard_map/all_to_all | solution.py:316
  172.8 2.7 %collective-permute-start.1 = (bf16[4,128,128]{2,1,0:T(8,128)(2,1)}, bf16[4,128,128]{2,1,0:T(8,128)(2,1)}, u32[]{:S(2)}, u32[]{:S(2)}) collective-permute-start(bf16[4,128,128]{2,1,0:T(8,128)(2,1)} %get-tuple-element.31.src_ref.refs_0_), channel_id=1, source_target_pairs={{0,2},{1,3},{2,0},{3,1},{4,6},{5,7},{6,4},{7,5},{8,10},{9,11},{10,... | collective-permute-start | bytes 393224 | tf_op jit(solution)/shard_map/ppermute | solution.py:271
  177.8 2.5 %copy-done.3 = bf16[161,128,128]{2,1,0:T(8,128)(2,1)S(1)} copy-done((bf16[161,128,128]{2,1,0:T(8,128)(2,1)S(1)}, bf16[161,128,128]{2,1,0:T(8,128)(2,1)}, u32[]{:S(2)}) %copy-start.3) | copy-done | bytes 5275672
  180.3 2.2 %own.3.part_ref = f32[16,128,128]{2,1,0:T(8,128)S(1)} custom-call(s32[448]{0:T(512)S(1)} %get-tuple-element.35.tile_ref, s32[448]{0:T(512)S(1)} %get-tuple-element.36.slab_ref, s32[112]{0:T(128)S(1)} %get-tuple-element.37.into_ref, s32[2]{0:T(128)S(1)} %copy-done.14, bf16[161,128,128]{2,1,0:T(8,128)(2,1)S(1)} %copy-done.3, ...), custom_call_target="tpu_custom_call" | custom-call | flops 671088640 | bytes 4194304 | tf_op jit(solution)/shard_map/own/pallas_call | solution.py:317
  182.6 15.6 %all-to-all-done.3.src_ref = bf16[64,128,128]{2,1,0:T(8,128)(2,1)S(1)} async-done(((bf16[64,128,128]{2,1,0:T(8,128)(2,1)}), bf16[64,128,128]{2,1,0:T(8,128)(2,1)S(1)}, u32[]{:S(2)}, u32[]{:S(2)}) %all-to-all-start.3) | async-done | bytes 2097184 | tf_op jit(solution)/shard_map/all_to_all | solution.py:316
  198.1 2.5 %copy-done.4 = bf16[161,128,128]{2,1,0:T(8,128)(2,1)S(1)} copy-done((bf16[161,128,128]{2,1,0:T(8,128)(2,1)S(1)}, bf16[161,128,128]{2,1,0:T(8,128)(2,1)}, u32[]{:S(2)}) %copy-start.4) | copy-done | bytes 5275672
  201.7 4.3 %far.3.refs_0_ = bf16[544,128]{1,0:T(8,128)(2,1)S(1)} custom-call(s32[448]{0:T(512)S(1)} %get-tuple-element.35.tile_ref, s32[448]{0:T(512)S(1)} %get-tuple-element.36.slab_ref, s32[112]{0:T(128)S(1)} %get-tuple-element.37.into_ref, s32[2]{0:T(128)S(1)} %copy-done.14, bf16[161,128,128]{2,1,0:T(8,128)(2,1)S(1)} %copy-done.4, ...), custom_call_target="tpu_custom_call" | custom-call | flops 671088640 | bytes 8388608 | tf_op jit(solution)/shard_map/far/pallas_call | solution.py:332
  205.9 2.4 %collective-permute-start.5 = (bf16[4,128,128]{2,1,0:T(8,128)(2,1)}, bf16[4,128,128]{2,1,0:T(8,128)(2,1)S(1)}, u32[]{:S(2)}, u32[]{:S(2)}) collective-permute-start(bf16[4,128,128]{2,1,0:T(8,128)(2,1)} %get-tuple-element.43.refs_4_.src_ref), channel_id=1, source_target_pairs={{0,3},{1,0},{2,1},{3,2},{4,7},{5,4},{6,5},{7,6},{8,11},{9,8},{10,9... | collective-permute-start | bytes 393224 | tf_op jit(solution)/shard_map/ppermute | solution.py:271
  208.4 1.7 collective-permute-start.7
  211.4 1.7 early.1.early_ref
  213.1 2.6 %collective-permute-done.6.refs_1_ = bf16[544,128]{1,0:T(8,128)(2,1)S(1)} collective-permute-done((bf16[544,128]{1,0:T(8,128)(2,1)S(1)}, bf16[544,128]{1,0:T(8,128)(2,1)S(1)}, u32[]{:S(2)}, u32[]{:S(2)}) %collective-permute-start.6) | collective-permute-done | bytes 139296 | tf_op jit(solution)/shard_map/ppermute | solution.py:271
  215.8 1.7 collective-permute-done.8.refs_3_
  217.5 1.2 final.1
  (57 shorter events, 13.1 us)
Async XLA Ops:
  0.0 211.2 %copy-start = (bf16[3,256,256]{2,1,0:T(8,128)(2,1)S(1)}, bf16[3,256,256]{2,1,0:T(8,128)(2,1)}, u32[]{:S(2)}) copy-start(bf16[3,256,256]{2,1,0:T(8,128)(2,1)} %param.15) | copy-start | bytes 1179652
  0.0 1.0 copy-start.11
  3.0 50.2 %all-to-all-start = ((bf16[8,4,128,128]{3,2,1,0:T(8,128)(2,1)}), bf16[8,4,128,128]{3,2,1,0:T(8,128)(2,1)S(1)}, u32[]{:S(2)}, u32[]{:S(2)}) async-start(bf16[8,4,128,128]{3,2,1,0:T(8,128)(2,1)} %get-tuple-element.29), calls=%async_computation | async-start | bytes 2097152 | tf_op jit(solution)/shard_map/all_to_all | solution.py:307
  53.2 8.0 %copy-start.15 = (s32[3]{0:T(128)}, s32[3]{0:T(128)S(1)}, u32[]{:S(2)}) copy-start(s32[3]{0:T(128)S(1)} %pad_add_fusion.me_ref) | copy-start | bytes 40
  59.9 1.3 copy-start.9
  61.2 37.0 %all-to-all-start.1 = ((bf16[64,128,128]{2,1,0:T(8,128)(2,1)}), bf16[64,128,128]{2,1,0:T(8,128)(2,1)S(1)}, u32[]{:S(2)}, u32[]{:S(2)}) async-start(bf16[64,128,128]{2,1,0:T(8,128)(2,1)} %copy-done.9), calls=%async_computation.1 | async-start | bytes 4194304 | tf_op jit(solution)/shard_map/all_to_all | solution.py:316
  72.6 2.5 %copy-start.5 = (bf16[160,128,128]{2,1,0:T(8,128)(2,1)S(1)}, bf16[160,128,128]{2,1,0:T(8,128)(2,1)}, u32[]{:S(2)}) copy-start(bf16[160,128,128]{2,1,0:T(8,128)(2,1)} %tiles_ref) | copy-start | bytes 15728644
  75.1 0.7 copy-start.19
  75.1 0.7 copy-start.20
  85.4 2.3 %copy-start.1 = (bf16[161,128,128]{2,1,0:T(8,128)(2,1)}, bf16[161,128,128]{2,1,0:T(8,128)(2,1)S(1)}, u32[]{:S(2)}) copy-start(bf16[161,128,128]{2,1,0:T(8,128)(2,1)S(1)} %stage.1.tiles_ref) | copy-start | bytes 15826948
  98.1 2.5 %copy-start.2 = (bf16[161,128,128]{2,1,0:T(8,128)(2,1)S(1)}, bf16[161,128,128]{2,1,0:T(8,128)(2,1)}, u32[]{:S(2)}) copy-start(bf16[161,128,128]{2,1,0:T(8,128)(2,1)} %copy-done.1) | copy-start | bytes 15826948
  100.6 1.0 copy-start.6
  101.7 0.6 copy-start.13
  107.7 1.0 copy-start.10
  109.3 46.2 %copy-start.16 = (s32[3]{0:T(128)S(1)}, s32[3]{0:T(128)}, u32[]{:S(2)}) copy-start(s32[3]{0:T(128)} %copy-done.15) | copy-start | bytes 40
  109.3 8.8 %copy-start.18 = (f32[8,128]{1,0:T(8,128)S(1)}, f32[8,128]{1,0:T(8,128)}, u32[]{:S(2)}) copy-start(f32[8,128]{1,0:T(8,128)} %copy-done.17) | copy-start | bytes 12292
  109.3 46.2 %all-to-all-start.2 = ((bf16[8,4,128,128]{3,2,1,0:T(8,128)(2,1)}), bf16[8,4,128,128]{3,2,1,0:T(8,128)(2,1)S(1)}, u32[]{:S(2)}, u32[]{:S(2)}) async-start(bf16[8,4,128,128]{3,2,1,0:T(8,128)(2,1)} %bitcast.17), calls=%async_computation.2 | async-start | bytes 2097152 | tf_op jit(solution)/shard_map/all_to_all | solution.py:307
  162.2 1.3 copy-start.8
  163.5 14.3 %copy-start.14 = (s32[2]{0:T(128)S(1)}, s32[2]{0:T(128)}, u32[]{:S(2)}) copy-start(s32[2]{0:T(128)} %copy-done.12) | copy-start | bytes 28
  163.5 34.6 %all-to-all-start.3 = ((bf16[64,128,128]{2,1,0:T(8,128)(2,1)}), bf16[64,128,128]{2,1,0:T(8,128)(2,1)S(1)}, u32[]{:S(2)}, u32[]{:S(2)}) async-start(bf16[64,128,128]{2,1,0:T(8,128)(2,1)} %copy-done.8), calls=%async_computation.3 | async-start | bytes 4194304 | tf_op jit(solution)/shard_map/all_to_all | solution.py:316
  171.9 34.0 %collective-permute-start = (bf16[4,128,128]{2,1,0:T(8,128)(2,1)}, bf16[4,128,128]{2,1,0:T(8,128)(2,1)}, u32[]{:S(2)}, u32[]{:S(2)}) collective-permute-start(bf16[4,128,128]{2,1,0:T(8,128)(2,1)} %get-tuple-element.31.src_ref.refs_0_), channel_id=1, source_target_pairs={{0,1},{1,2},{2,3},{3,0},{4,5},{5,6},{6,7},{7,4},{8,9},{9,10},{10,1... | collective-permute-start | bytes 393224 | tf_op jit(solution)/shard_map/ppermute | solution.py:271
  172.8 35.6 %collective-permute-start.1 = (bf16[4,128,128]{2,1,0:T(8,128)(2,1)}, bf16[4,128,128]{2,1,0:T(8,128)(2,1)}, u32[]{:S(2)}, u32[]{:S(2)}) collective-permute-start(bf16[4,128,128]{2,1,0:T(8,128)(2,1)} %get-tuple-element.31.src_ref.refs_0_), channel_id=1, source_target_pairs={{0,2},{1,3},{2,0},{3,1},{4,6},{5,7},{6,4},{7,5},{8,10},{9,11},{10,... | collective-permute-start | bytes 393224 | tf_op jit(solution)/shard_map/ppermute | solution.py:271
  175.5 32.9 %collective-permute-start.2 = (bf16[4,128,128]{2,1,0:T(8,128)(2,1)}, bf16[4,128,128]{2,1,0:T(8,128)(2,1)}, u32[]{:S(2)}, u32[]{:S(2)}) collective-permute-start(bf16[4,128,128]{2,1,0:T(8,128)(2,1)} %get-tuple-element.31.src_ref.refs_0_), channel_id=1, source_target_pairs={{0,3},{1,0},{2,1},{3,2},{4,7},{5,4},{6,5},{7,6},{8,11},{9,8},{10,9... | collective-permute-start | bytes 393224 | tf_op jit(solution)/shard_map/ppermute | solution.py:271
  176.6 33.5 %collective-permute-start.3 = (bf16[4,128,128]{2,1,0:T(8,128)(2,1)}, bf16[4,128,128]{2,1,0:T(8,128)(2,1)}, u32[]{:S(2)}, u32[]{:S(2)}) collective-permute-start(bf16[4,128,128]{2,1,0:T(8,128)(2,1)} %get-tuple-element.43.refs_4_.src_ref), channel_id=1, source_target_pairs={{0,1},{1,2},{2,3},{3,0},{4,5},{5,6},{6,7},{7,4},{8,9},{9,10},{10,1... | collective-permute-start | bytes 393224 | tf_op jit(solution)/shard_map/ppermute | solution.py:271
  177.0 34.5 %collective-permute-start.4 = (bf16[4,128,128]{2,1,0:T(8,128)(2,1)}, bf16[4,128,128]{2,1,0:T(8,128)(2,1)}, u32[]{:S(2)}, u32[]{:S(2)}) collective-permute-start(bf16[4,128,128]{2,1,0:T(8,128)(2,1)} %get-tuple-element.43.refs_4_.src_ref), channel_id=1, source_target_pairs={{0,2},{1,3},{2,0},{3,1},{4,6},{5,7},{6,4},{7,5},{8,10},{9,11},{10,... | collective-permute-start | bytes 393224 | tf_op jit(solution)/shard_map/ppermute | solution.py:271
  177.8 2.5 %copy-start.3 = (bf16[161,128,128]{2,1,0:T(8,128)(2,1)S(1)}, bf16[161,128,128]{2,1,0:T(8,128)(2,1)}, u32[]{:S(2)}) copy-start(bf16[161,128,128]{2,1,0:T(8,128)(2,1)} %copy-done.1) | copy-start | bytes 15826948
  198.1 2.5 %copy-start.4 = (bf16[161,128,128]{2,1,0:T(8,128)(2,1)S(1)}, bf16[161,128,128]{2,1,0:T(8,128)(2,1)}, u32[]{:S(2)}) copy-start(bf16[161,128,128]{2,1,0:T(8,128)(2,1)} %copy-done.1) | copy-start | bytes 15826948
  200.6 1.0 copy-start.7
  205.9 5.5 %collective-permute-start.5 = (bf16[4,128,128]{2,1,0:T(8,128)(2,1)}, bf16[4,128,128]{2,1,0:T(8,128)(2,1)S(1)}, u32[]{:S(2)}, u32[]{:S(2)}) collective-permute-start(bf16[4,128,128]{2,1,0:T(8,128)(2,1)} %get-tuple-element.43.refs_4_.src_ref), channel_id=1, source_target_pairs={{0,3},{1,0},{2,1},{3,2},{4,7},{5,4},{6,5},{7,6},{8,11},{9,8},{10,9... | collective-permute-start | bytes 393224 | tf_op jit(solution)/shard_map/ppermute | solution.py:271
  208.4 7.4 %collective-permute-start.6 = (bf16[544,128]{1,0:T(8,128)(2,1)S(1)}, bf16[544,128]{1,0:T(8,128)(2,1)S(1)}, u32[]{:S(2)}, u32[]{:S(2)}) collective-permute-start(bf16[544,128]{1,0:T(8,128)(2,1)S(1)} %far.3.refs_0_), channel_id=1, source_target_pairs={{0,1},{1,2},{2,3},{3,0},{4,5},{5,6},{6,7},{7,4},{8,9},{9,10},{10,1... | collective-permute-start | bytes 417800 | tf_op jit(solution)/shard_map/ppermute | solution.py:271
  208.4 7.4 %collective-permute-start.7 = (bf16[544,128]{1,0:T(8,128)(2,1)S(1)}, bf16[544,128]{1,0:T(8,128)(2,1)S(1)}, u32[]{:S(2)}, u32[]{:S(2)}) collective-permute-start(bf16[544,128]{1,0:T(8,128)(2,1)S(1)} %far.3.refs_0_), channel_id=1, source_target_pairs={{0,2},{1,3},{2,0},{3,1},{4,6},{5,7},{6,4},{7,5},{8,10},{9,11},{10,... | collective-permute-start | bytes 417800 | tf_op jit(solution)/shard_map/ppermute | solution.py:271
  210.1 7.4 %collective-permute-start.8 = (bf16[544,128]{1,0:T(8,128)(2,1)S(1)}, bf16[544,128]{1,0:T(8,128)(2,1)S(1)}, u32[]{:S(2)}, u32[]{:S(2)}) collective-permute-start(bf16[544,128]{1,0:T(8,128)(2,1)S(1)} %far.3.refs_0_), channel_id=1, source_target_pairs={{0,3},{1,0},{2,1},{3,2},{4,7},{5,4},{6,5},{7,6},{8,11},{9,8},{10,9... | collective-permute-start | bytes 417800 | tf_op jit(solution)/shard_map/ppermute | solution.py:271
  (2 other events, 1.1 us)
